TPU v7x, 512 devices: a whole 4x4x16 slice. The times are simulated.
512 devices in a mesh: tile: 32 (over y, x, core), depth: 16 (over z).
Axes of the slice: x: 4, y: 4, z: 16, core: 2. Of those that a mesh axis runs over, the one named last changes fastest.
Arguments:
- features: bfloat16 [16, 8192, 128], P('depth', 'tile'), may hold values from -4 to 4
- logits: float32 [16, 8192], P('depth', 'tile'), may hold values from -2.75 to 5.5
- geometry: float32 [2, 16, 5, 8192], P(None, 'depth', None, 'tile'), may hold values from -0.6 to 32, as said below
- dest_slot: int32 [2, 16, 8192], P(None, 'depth', 'tile'), may hold values from -1 to 8191, as said below
- target: bfloat16 [2, 64, 128, 1024], P(None, 'tile'), may hold values from -3 to 3
Outputs:
- images: bfloat16 [2, 64, 128, 1024], P(None, 'tile', None, 'depth')
- new_features: bfloat16 [16, 8192, 128], P('depth', 'tile')
- new_logits: float32 [16, 8192], P('depth', 'tile')
- shape_grads: float32 [2, 16, 5, 8192], P(None, 'depth', None, 'tile')
Inputs may be any that keep to these rules, and one draw needn't show every extreme that they name: `dest_slot`: for each view and layer no two splats share a slot; -1 marks a splat outside the view; a splat's place within its tile is its front-to-back order. At most 8 splats of one layer held by one index of tile go to the tiles of one index of tile, and in every view and layer there is an index of tile whose tiles receive exactly 8 from every owner, so that all their slots are used. `geometry`: components 0 and 1 are a splat's centre in pixels within its tile, from 0 to 32; components 2 and 3 lie in -0.5 to 2.0; component 4 in -0.6 to 0.6.
All inputs are finite; a program needn't handle non-finite values.
Results may differ from a plain program's by a relative error of at most 0.0073.
Values may be sent and summed in bfloat16 or wider, within the bound.
No kernel may reach another device: no remote copies, remote signals or barrier semaphores. Data moves between devices by JAX's collectives and lax.ppermute only.
A program may use at most 64 MiB of HBM per device.

v0:
```python
from functools import partial

import jax
import jax.numpy as jnp
from jax import lax
from jax.sharding import PartitionSpec as P

F = 128
W = 32
S = 128
VIEWS = 2
P_SIZE = 1024


clamp_top = 0.99
feature_rate = 0.5
opacity_rate = 0.5


def split_up(shard, dim, size):
    shape = shard.shape
    tiles = shard.reshape(*shape[:dim], size, shape[dim] // size, *shape[dim + 1 :])
    return jnp.moveaxis(tiles, dim, 0)


def sent_and_summed(shard, axis, dim):
    tiles = split_up(shard, dim, lax.axis_size(axis))
    arrived = lax.all_to_all(tiles, axis, split_axis=0, concat_axis=0, tiled=True)
    return arrived.astype(jnp.float32).sum(axis=0)


def joined_along(tiles, dim):
    tiles = jnp.moveaxis(tiles, 0, dim)
    shape = tiles.shape
    return tiles.reshape(*shape[:dim], shape[dim] * shape[dim + 1], *shape[dim + 2 :])


def from_everyone(shard, axis):
    copies = jnp.broadcast_to(shard, (lax.axis_size(axis), *shard.shape))
    return lax.all_to_all(copies, axis, split_axis=0, concat_axis=0, tiled=True)


def gather_directly(shard, axis, dim):
    return joined_along(from_everyone(shard, axis), dim)


def pixel_places():
    places = jnp.arange(P_SIZE, dtype=jnp.int32)
    across = (places % W).astype(jnp.float32) + 0.5
    downward = (places // W).astype(jnp.float32) + 0.5
    return (across, downward)


def block_sum(values, reverse):
    length = values.shape[0]
    block_rows = min(128, length)
    blocks = values.reshape(length // block_rows, block_rows, values.shape[1])
    positions = jnp.arange(block_rows)
    if reverse:
        triangle = (positions[:, None] < positions[None, :]).astype(jnp.float32)
    else:
        triangle = (positions[:, None] > positions[None, :]).astype(jnp.float32)
    within = jnp.einsum("ij,bjp->bip", triangle, blocks, precision=lax.Precision.HIGHEST)
    block_totals = jnp.sum(blocks, axis=1)
    if reverse:
        offsets = jnp.sum(block_totals, axis=0)[None, :] - jnp.cumsum(block_totals, axis=0)
    else:
        offsets = jnp.cumsum(block_totals, axis=0) - block_totals
    return (within + offsets[:, None, :]).reshape(length, values.shape[1])


def splat_fields(shapes):
    across, downward = pixel_places()
    delta_x = across[None, :] - shapes[0][:, None]
    delta_y = downward[None, :] - shapes[1][:, None]
    coef_a = jnp.exp(shapes[2])[:, None]
    coef_c = jnp.exp(shapes[3])[:, None]
    spread = jnp.exp(0.5 * (shapes[2] + shapes[3]))[:, None]
    coef_b = shapes[4][:, None] * spread
    quadric = (
        coef_a * delta_x * delta_x + 2.0 * coef_b * delta_x * delta_y + coef_c * delta_y * delta_y
    )
    falloff = jnp.exp(-0.5 * quadric)
    opacity = shapes[5][:, None]
    product = opacity * falloff
    coverage = jnp.minimum(product, clamp_top)
    return (delta_x, delta_y, coef_a, coef_b, coef_c, spread, falloff, opacity, product, coverage)


def layer_forward(inputs):
    slot_feats, shapes = inputs
    coverage = splat_fields(shapes)[9]
    log_keep = jnp.log(1.0 - coverage)
    before = block_sum(log_keep, False)
    weights = (coverage * jnp.exp(before)).astype(jnp.bfloat16)
    composite = lax.dot_general(
        slot_feats, weights, (((0,), (0,)), ((), ())), preferred_element_type=jnp.float32
    )
    layer_keep = jnp.exp(jnp.sum(log_keep, axis=0))
    return (composite, layer_keep)


def layer_backward(inputs):
    slot_feats, shapes, grad_comp, grad_keep = inputs
    delta_x, delta_y, coef_a, coef_b, coef_c, spread, falloff, opacity, product, coverage = (
        splat_fields(shapes)
    )
    log_keep = jnp.log(1.0 - coverage)
    before = block_sum(log_keep, False)
    decayed = jnp.exp(before)
    exact_weight = coverage * decayed
    weights = exact_weight.astype(jnp.bfloat16)
    layer_keep = jnp.exp(jnp.sum(log_keep, axis=0))
    grad_feat = lax.dot_general(
        weights, grad_comp, (((1,), (1,)), ((), ())), preferred_element_type=jnp.float32
    )
    grad_weight = jnp.dot(slot_feats, grad_comp, preferred_element_type=jnp.float32)
    grad_before = grad_weight * exact_weight
    later = block_sum(grad_before, True)
    grad_log = later + (grad_keep * layer_keep)[None, :]
    grad_coverage = grad_weight * decayed - grad_log / (1.0 - coverage)
    grad_product = jnp.where(product < clamp_top, grad_coverage, 0.0)
    grad_quadric = -0.5 * opacity * falloff * grad_product
    grad_mean_x = -2.0 * jnp.sum(grad_quadric * (coef_a * delta_x + coef_b * delta_y), axis=1)
    grad_mean_y = -2.0 * jnp.sum(grad_quadric * (coef_b * delta_x + coef_c * delta_y), axis=1)
    grad_first = jnp.sum(grad_quadric * delta_x * delta_x, axis=1)
    grad_cross = jnp.sum(grad_quadric * 2.0 * delta_x * delta_y, axis=1)
    grad_second = jnp.sum(grad_quadric * delta_y * delta_y, axis=1)
    grad_log_a = coef_a[:, 0] * grad_first + 0.5 * coef_b[:, 0] * grad_cross
    grad_log_c = coef_c[:, 0] * grad_second + 0.5 * coef_b[:, 0] * grad_cross
    grad_corr = spread[:, 0] * grad_cross
    opacity_flat = opacity[:, 0]
    grad_logit = opacity_flat * (1.0 - opacity_flat) * jnp.sum(falloff * grad_product, axis=1)
    grad_shape = jnp.stack(
        [grad_mean_x, grad_mean_y, grad_log_a, grad_log_c, grad_corr, grad_logit]
    )
    return (grad_feat, grad_shape)


def rear_step(all_keeps, all_terms, depth_here, layers, counter, carried):
    layer_at = layers - 1 - counter
    updated = all_terms[layer_at] + all_keeps[layer_at] * carried
    return jnp.where(layer_at > depth_here, updated, carried)


def body(features, logits, geometry, dest_slot, target):
    owners = lax.axis_size("tile")
    layers = lax.axis_size("depth")
    depth_here = lax.axis_index("depth")
    tiles_here = target.shape[1]
    owned = features.shape[1]
    capacity = owned // owners
    pixel_share = P_SIZE // layers
    splat_feats = features[0]
    logit_now = logits[0]
    images = []
    shape_grads = []
    for view_index in range(VIEWS):
        slot_ids = dest_slot[view_index, 0]
        visible = slot_ids >= 0
        receiver = jnp.where(visible, slot_ids // owned, owners)
        matches = (receiver[:, None] == jnp.arange(owners, dtype=jnp.int32)[None, :]).astype(
            jnp.int32
        )
        place_in = jnp.sum((jnp.cumsum(matches, axis=0) - matches) * matches, axis=1)
        position = jnp.where(visible, receiver * capacity + place_in, owners * capacity)
        local_slot = jnp.where(visible, slot_ids - receiver * owned, -1)
        opacity = jax.nn.sigmoid(logit_now)
        shape_rows = jnp.concatenate([geometry[view_index, 0], opacity[None, :]], axis=0).T
        row_buffer = (
            jnp.zeros((owners * capacity + 1, F), jnp.bfloat16)
            .at[position]
            .set(splat_feats)[:-1]
            .reshape(owners, capacity, F)
        )
        slot_buffer = (
            jnp.full((owners * capacity + 1,), -1, jnp.int32)
            .at[position]
            .set(local_slot)[:-1]
            .reshape(owners, capacity)
        )
        shape_buffer = (
            jnp.zeros((owners * capacity + 1, 6), jnp.float32)
            .at[position]
            .set(shape_rows)[:-1]
            .reshape(owners, capacity, 6)
        )
        got_rows, got_slots = (
            lax.all_to_all(row_buffer, "tile", split_axis=0, concat_axis=0, tiled=True),
            lax.all_to_all(slot_buffer, "tile", split_axis=0, concat_axis=0, tiled=True),
        )
        got_shapes = lax.all_to_all(shape_buffer, "tile", split_axis=0, concat_axis=0, tiled=True)
        arrived = got_slots.reshape(-1)
        present = arrived >= 0
        landing = jnp.where(present, arrived, owned)
        slot_feats = (
            jnp.zeros((owned + 1, F), jnp.bfloat16)
            .at[landing]
            .set(got_rows.reshape(-1, F))[:-1]
            .reshape(tiles_here, S, F)
        )
        slot_shapes = (
            jnp.zeros((owned + 1, 6), jnp.float32)
            .at[landing]
            .set(got_shapes.reshape(-1, 6))[:-1]
            .reshape(tiles_here, S, 6)
            .transpose(0, 2, 1)
        )
        composites, layer_keeps = lax.map(layer_forward, (slot_feats, slot_shapes))
        all_keeps = lax.all_gather(layer_keeps[None], "depth", axis=0, tiled=True)
        earlier_mask = (jnp.arange(layers) < depth_here)[:, None, None]
        ahead = jnp.prod(jnp.where(earlier_mask, all_keeps, 1.0), axis=0)
        contrib = ahead[:, None, :] * composites
        image_part = sent_and_summed(contrib.astype(jnp.bfloat16), "depth", 2)
        target_part = lax.dynamic_slice_in_dim(
            target[view_index], depth_here * pixel_share, pixel_share, 2
        ).astype(jnp.float32)
        residual = gather_directly(image_part - target_part, "depth", 2)
        images.append(image_part.astype(jnp.bfloat16))
        pixel_terms = jnp.sum(residual * composites, axis=1)
        all_terms = gather_directly(pixel_terms[None], "depth", 0)
        behind = lax.fori_loop(
            0,
            layers,
            partial(rear_step, all_keeps, all_terms, depth_here, layers),
            jnp.zeros_like(pixel_terms),
        )
        grad_keep = ahead * behind
        grad_comp = (ahead[:, None, :] * residual).astype(jnp.bfloat16)
        grad_feat, grad_shape = lax.map(
            layer_backward, (slot_feats, slot_shapes, grad_comp, grad_keep)
        )
        flat_feat = grad_feat.reshape(owned, F)
        flat_shape = grad_shape.transpose(0, 2, 1).reshape(owned, 6)
        fetched = jnp.where(present, arrived, 0)
        back_feat = jnp.where(present[:, None], flat_feat[fetched], 0.0).reshape(
            owners, capacity, F
        )
        back_shape = jnp.where(present[:, None], flat_shape[fetched], 0.0).reshape(
            owners, capacity, 6
        )
        return_feat, return_shape = (
            lax.all_to_all(back_feat, "tile", split_axis=0, concat_axis=0, tiled=True),
            lax.all_to_all(back_shape, "tile", split_axis=0, concat_axis=0, tiled=True),
        )
        padded_feat = jnp.concatenate(
            [return_feat.reshape(-1, F), jnp.zeros((1, F), jnp.float32)], axis=0
        )
        padded_shape = jnp.concatenate(
            [return_shape.reshape(-1, 6), jnp.zeros((1, 6), jnp.float32)], axis=0
        )
        splat_grad_feat = padded_feat[position]
        splat_grad_shape = padded_shape[position]
        shape_grads.append(splat_grad_shape[:, :5].T)
        splat_feats = (splat_feats.astype(jnp.float32) - feature_rate * splat_grad_feat).astype(
            jnp.bfloat16
        )
        logit_now = logit_now - opacity_rate * splat_grad_shape[:, 5]
    return (jnp.stack(images), splat_feats[None], logit_now[None], jnp.stack(shape_grads)[:, None])


def solution(mesh):
    placed = (
        P("depth", "tile", None),
        P("depth", "tile"),
        P(None, "depth", None, "tile"),
        P(None, "depth", "tile"),
        P(None, "tile", None, None),
    )
    return jax.shard_map(
        body,
        mesh=mesh,
        in_specs=placed,
        out_specs=(
            P(None, "tile", None, "depth"),
            P("depth", "tile", None),
            P("depth", "tile"),
            P(None, "depth", None, "tile"),
        ),
        check_vma=False,
    )
```

profile of v0, /device:TPU:1, one launch (start us, length us, event | category | flops | bytes accessed | tf_op | source)
XLA Modules:
  0.0 448.0 jit_solution(14896957817625969627)
XLA Ops:
  8.6 10.4 %all-to-all-start = ((s32[32,1,8]{2,1,0:T(1,128)}), s32[32,1,8]{2,1,0:T(1,128)S(1)}, u32[]{:S(2)}, u32[]{:S(2)}) async-start(s32[32,1,8]{2,1,0:T(1,128)} %bitcast.92), calls=%async_computation | async-start | bytes 32768 | tf_op jit(solution)/shard_map/all_to_all | solution.py:190
  26.1 5.2 %all-to-all-start.2 = ((f32[32,8,6]{2,1,0:T(8,128)}), f32[32,8,6]{2,1,0:T(8,128)S(1)}, u32[]{:S(2)}, u32[]{:S(2)}) async-start(f32[32,8,6]{2,1,0:T(8,128)} %slice_bitcast_fusion.15), calls=%async_computation.2 | async-start | bytes 262144 | tf_op jit(solution)/shard_map/all_to_all | solution.py:192
  32.6 6.3 %all-to-all-done.2 = f32[32,8,6]{2,1,0:T(8,128)S(1)} async-done(((f32[32,8,6]{2,1,0:T(8,128)}), f32[32,8,6]{2,1,0:T(8,128)S(1)}, u32[]{:S(2)}, u32[]{:S(2)}) %all-to-all-start.2) | async-done | bytes 6176 | tf_op jit(solution)/shard_map/all_to_all | solution.py:192
  44.1 6.2 %all-to-all-done.1 = bf16[32,8,128]{2,1,0:T(8,128)(2,1)S(1)} async-done(((bf16[32,8,128]{2,1,0:T(8,128)(2,1)}), bf16[32,8,128]{2,1,0:T(8,128)(2,1)S(1)}, u32[]{:S(2)}, u32[]{:S(2)}) %all-to-all-start.1) | async-done | bytes 65568 | tf_op jit(solution)/shard_map/all_to_all | solution.py:189
  52.9 5.0 %while.88 = (s32[]{:T(128)}, f32[2,128,1024]{1,2,0:T(8,128)S(1)}, f32[2,1024]{1,0:T(2,128)S(1)}, bf16[2,128,128]{2,1,0:T(8,128)(2,1)S(1)}, f32[2,6,128]{2,1,0:T(8,128)S(1)}, /*index=5*/s32[]{:T(128)}, s32[]{:T(128)}) while((s32[]{:T(128)}, f32[2,128,1024]{1,2,0:T(8,128)S(1)}, f32[2,1024]{1,0:T(2,128)S(1)}, ...), condition=%wide.region_11.12_spmd, body=%wide.region_8.11_spmd.sunk | while | flops 242777600 | bytes 1177685 | solution.py:209
  57.9 27.0 %all-gather.2 = f32[16,2,1024]{2,1,0:T(2,128)S(1)} all-gather(f32[1,2,1024]{2,1,0:T(2,128)S(1)} %bitcast.719), channel_id=2, replica_groups=mesh['tile'=32,'depth'=16] {'depth'}, dimensions={0}, use_global_device_ids=true | all-gather | bytes 139264 | tf_op jit(solution)/shard_map/all_gather | solution.py:210
  86.2 6.7 %all-to-all-start.3 = ((bf16[16,2,128,64]{2,3,1,0:T(8,128)(2,1)}), bf16[16,2,128,64]{2,3,1,0:T(8,128)(2,1)S(1)}, u32[]{:S(2)}, u32[]{:S(2)}) async-start(bf16[16,2,128,64]{2,3,1,0:T(8,128)(2,1)} %copy.118), calls=%async_computation.3 | async-start | bytes 1048576 | tf_op jit(solution)/shard_map/all_to_all | solution.py:28
  93.2 18.2 %all-to-all-done.3 = bf16[16,2,128,64]{2,3,1,0:T(8,128)(2,1)S(1)} async-done(((bf16[16,2,128,64]{2,3,1,0:T(8,128)(2,1)}), bf16[16,2,128,64]{2,3,1,0:T(8,128)(2,1)S(1)}, u32[]{:S(2)}, u32[]{:S(2)}) %all-to-all-start.3) | async-done | bytes 524320 | tf_op jit(solution)/shard_map/all_to_all | solution.py:28
  112.7 13.6 %all-to-all-start.5 = ((f32[16,2,128,64]{2,3,1,0:T(8,128)}), f32[16,2,128,64]{2,3,1,0:T(8,128)S(1)}, u32[]{:S(2)}, u32[]{:S(2)}) async-start(f32[16,2,128,64]{2,3,1,0:T(8,128)} %broadcast_in_dim.232), calls=%async_computation.5 | async-start | bytes 2097152 | tf_op jit(solution)/shard_map/all_to_all | solution.py:40
  128.4 42.7 %all-to-all-done.5 = f32[16,2,128,64]{2,3,1,0:T(8,128)S(1)} async-done(((f32[16,2,128,64]{2,3,1,0:T(8,128)}), f32[16,2,128,64]{2,3,1,0:T(8,128)S(1)}, u32[]{:S(2)}, u32[]{:S(2)}) %all-to-all-start.5) | async-done | bytes 1048608 | tf_op jit(solution)/shard_map/all_to_all | solution.py:40
  171.1 8.5 %all-to-all-start.4 = ((s32[32,1,8]{2,1,0:T(1,128)}), s32[32,1,8]{2,1,0:T(1,128)S(1)}, u32[]{:S(2)}, u32[]{:S(2)}) async-start(s32[32,1,8]{2,1,0:T(1,128)} %bitcast.113), calls=%async_computation.4 | async-start | bytes 32768 | tf_op jit(solution)/shard_map/all_to_all | solution.py:190
  180.4 6.2 %all-to-all-done.4 = s32[32,1,8]{2,1,0:T(1,128)S(1)} async-done(((s32[32,1,8]{2,1,0:T(1,128)}), s32[32,1,8]{2,1,0:T(1,128)S(1)}, u32[]{:S(2)}, u32[]{:S(2)}) %all-to-all-start.4) | async-done | bytes 1056 | tf_op jit(solution)/shard_map/all_to_all | solution.py:190
  187.3 8.8 %all-to-all-start.6 = ((f32[16,1,2,1024]{3,2,1,0:T(2,128)}), f32[16,1,2,1024]{3,2,1,0:T(2,128)S(1)}, u32[]{:S(2)}, u32[]{:S(2)}) async-start(f32[16,1,2,1024]{3,2,1,0:T(2,128)} %broadcast_in_dim.233), calls=%async_computation.6 | async-start | bytes 262144 | tf_op jit(solution)/shard_map/all_to_all | solution.py:40
  197.1 11.0 %all-to-all-done.6 = f32[16,1,2,1024]{3,2,1,0:T(2,128)S(1)} async-done(((f32[16,1,2,1024]{3,2,1,0:T(2,128)}), f32[16,1,2,1024]{3,2,1,0:T(2,128)S(1)}, u32[]{:S(2)}, u32[]{:S(2)}) %all-to-all-start.6) | async-done | bytes 131104 | tf_op jit(solution)/shard_map/all_to_all | solution.py:40
  209.0 9.3 %while.89 = (s32[]{:T(128)}, f32[2,128,128]{2,1,0:T(8,128)S(1)}, f32[2,6,128]{2,1,0:T(8,128)S(1)}, f32[2,6,128]{2,1,0:T(8,128)S(1)}, bf16[2,128,1024]{1,2,0:T(8,...) while((s32[]{:T(128)}, f32[2,128,128]{2,1,0:T(8,128)S(1)}, ...), condition=%wide.region_31.32_spmd, body=%wide.region_21.31_spmd.sunk | while | flops 485672448 | bytes 3947105 | solution.py:230
  219.9 7.2 %all-to-all-start.9 = ((f32[32,8,6]{2,1,0:T(8,128)}), f32[32,8,6]{2,1,0:T(8,128)S(1)}, u32[]{:S(2)}, u32[]{:S(2)}) async-start(f32[32,8,6]{2,1,0:T(8,128)} %bitcast_select_fusion.2), calls=%async_computation.9 | async-start | bytes 262144 | tf_op jit(solution)/shard_map/all_to_all | solution.py:244
  228.6 6.2 %all-to-all-done.9 = f32[32,8,6]{2,1,0:T(8,128)S(1)} async-done(((f32[32,8,6]{2,1,0:T(8,128)}), f32[32,8,6]{2,1,0:T(8,128)S(1)}, u32[]{:S(2)}, u32[]{:S(2)}) %all-to-all-start.9) | async-done | bytes 6176 | tf_op jit(solution)/shard_map/all_to_all | solution.py:244
  241.7 4.8 %all-to-all-done.7 = f32[32,8,128]{2,1,0:T(8,128)S(1)} async-done(((f32[32,8,128]{2,1,0:T(8,128)}), f32[32,8,128]{2,1,0:T(8,128)S(1)}, u32[]{:S(2)}, u32[]{:S(2)}) %all-to-all-start.7) | async-done | bytes 131104 | tf_op jit(solution)/shard_map/all_to_all | solution.py:243
  253.0 5.1 %all-to-all-done.10 = f32[32,8,6]{2,1,0:T(8,128)S(1)} async-done(((f32[32,8,6]{2,1,0:T(8,128)}), f32[32,8,6]{2,1,0:T(8,128)S(1)}, u32[]{:S(2)}, u32[]{:S(2)}) %all-to-all-start.10) | async-done | bytes 6176 | tf_op jit(solution)/shard_map/all_to_all | solution.py:192
  263.3 6.2 %all-to-all-done.8 = bf16[32,8,128]{2,1,0:T(8,128)(2,1)S(1)} async-done(((bf16[32,8,128]{2,1,0:T(8,128)(2,1)}), bf16[32,8,128]{2,1,0:T(8,128)(2,1)S(1)}, u32[]{:S(2)}, u32[]{:S(2)}) %all-to-all-start.8) | async-done | bytes 65568 | tf_op jit(solution)/shard_map/all_to_all | solution.py:189
  272.1 5.0 %while.90 = (s32[]{:T(128)}, f32[2,128,1024]{1,2,0:T(8,128)S(1)}, f32[2,1024]{1,0:T(2,128)S(1)}, bf16[2,128,128]{2,1,0:T(8,128)(2,1)S(1)}, f32[2,6,128]{2,1,0:T(8,128)S(1)}, /*index=5*/s32[]{:T(128)}, s32[]{:T(128)}) while((s32[]{:T(128)}, f32[2,128,1024]{1,2,0:T(8,128)S(1)}, f32[2,1024]{1,0:T(2,128)S(1)}, ...), condition=%wide.region_39.40_spmd, body=%wide.region_36.39_spmd.sunk | while | flops 242777600 | bytes 1177685 | solution.py:209
  277.1 21.9 %all-gather.3 = f32[16,2,1024]{2,1,0:T(2,128)S(1)} all-gather(f32[1,2,1024]{2,1,0:T(2,128)S(1)} %bitcast.721), channel_id=3, replica_groups=mesh['tile'=32,'depth'=16] {'depth'}, dimensions={0}, use_global_device_ids=true | all-gather | bytes 139264 | tf_op jit(solution)/shard_map/all_gather | solution.py:210
  300.3 4.1 all-to-all-start.11
  304.6 18.2 %all-to-all-done.11 = bf16[16,2,128,64]{2,3,1,0:T(8,128)(2,1)S(1)} async-done(((bf16[16,2,128,64]{2,3,1,0:T(8,128)(2,1)}), bf16[16,2,128,64]{2,3,1,0:T(8,128)(2,1)S(1)}, u32[]{:S(2)}, u32[]{:S(2)}) %all-to-all-start.11) | async-done | bytes 524320 | tf_op jit(solution)/shard_map/all_to_all | solution.py:28
  324.0 13.6 %all-to-all-start.12 = ((f32[16,2,128,64]{2,3,1,0:T(8,128)}), f32[16,2,128,64]{2,3,1,0:T(8,128)S(1)}, u32[]{:S(2)}, u32[]{:S(2)}) async-start(f32[16,2,128,64]{2,3,1,0:T(8,128)} %broadcast_in_dim.239), calls=%async_computation.12 | async-start | bytes 2097152 | tf_op jit(solution)/shard_map/all_to_all | solution.py:40
  337.7 44.8 %all-to-all-done.12 = f32[16,2,128,64]{2,3,1,0:T(8,128)S(1)} async-done(((f32[16,2,128,64]{2,3,1,0:T(8,128)}), f32[16,2,128,64]{2,3,1,0:T(8,128)S(1)}, u32[]{:S(2)}, u32[]{:S(2)}) %all-to-all-start.12) | async-done | bytes 1048608 | tf_op jit(solution)/shard_map/all_to_all | solution.py:40
  383.9 12.4 %all-to-all-start.13 = ((f32[16,1,2,1024]{3,2,1,0:T(2,128)}), f32[16,1,2,1024]{3,2,1,0:T(2,128)S(1)}, u32[]{:S(2)}, u32[]{:S(2)}) async-start(f32[16,1,2,1024]{3,2,1,0:T(2,128)} %broadcast_in_dim.240), calls=%async_computation.13 | async-start | bytes 262144 | tf_op jit(solution)/shard_map/all_to_all | solution.py:40
  397.2 11.1 %all-to-all-done.13 = f32[16,1,2,1024]{3,2,1,0:T(2,128)S(1)} async-done(((f32[16,1,2,1024]{3,2,1,0:T(2,128)}), f32[16,1,2,1024]{3,2,1,0:T(2,128)S(1)}, u32[]{:S(2)}, u32[]{:S(2)}) %all-to-all-start.13) | async-done | bytes 131104 | tf_op jit(solution)/shard_map/all_to_all | solution.py:40
  409.2 9.1 %while.91 = (s32[]{:T(128)}, f32[2,128,128]{2,1,0:T(8,128)S(1)}, f32[2,6,128]{2,1,0:T(8,128)S(1)}, f32[2,6,128]{2,1,0:T(8,128)S(1)}, bf16[2,128,1024]{1,2,0:T(8,...) while((s32[]{:T(128)}, f32[2,128,128]{2,1,0:T(8,128)S(1)}, ...), condition=%wide.region_55.56_spmd, body=%wide.region_45.55_spmd.sunk | while | flops 485672448 | bytes 3947105 | solution.py:230
  419.9 7.3 %all-to-all-start.15 = ((f32[32,8,6]{2,1,0:T(8,128)}), f32[32,8,6]{2,1,0:T(8,128)S(1)}, u32[]{:S(2)}, u32[]{:S(2)}) async-start(f32[32,8,6]{2,1,0:T(8,128)} %bitcast_select_fusion), calls=%async_computation.15 | async-start | bytes 262144 | tf_op jit(solution)/shard_map/all_to_all | solution.py:244
  428.7 6.2 %all-to-all-done.15 = f32[32,8,6]{2,1,0:T(8,128)S(1)} async-done(((f32[32,8,6]{2,1,0:T(8,128)}), f32[32,8,6]{2,1,0:T(8,128)S(1)}, u32[]{:S(2)}, u32[]{:S(2)}) %all-to-all-start.15) | async-done | bytes 6176 | tf_op jit(solution)/shard_map/all_to_all | solution.py:244
  441.1 5.5 %all-to-all-done.14 = f32[32,8,128]{2,1,0:T(8,128)S(1)} async-done(((f32[32,8,128]{2,1,0:T(8,128)}), f32[32,8,128]{2,1,0:T(8,128)S(1)}, u32[]{:S(2)}, u32[]{:S(2)}) %all-to-all-start.14) | async-done | bytes 131104 | tf_op jit(solution)/shard_map/all_to_all | solution.py:243
  (306 shorter events, 100.9 us)
Async XLA Ops:
  2.2 0.6 copy-start.6
  3.6 0.6 copy-start.7
  4.2 0.7 slice-start.2
  5.0 0.7 slice-start.3
  5.8 0.7 copy-start.5
  8.6 10.5 %copy-start.4 = (f32[2,1,5,256]{3,1,2,0:T(1,128)S(1)}, f32[2,1,5,256]{3,1,2,0:T(1,128)}, u32[]{:S(2)}) copy-start(f32[2,1,5,256]{3,1,2,0:T(1,128)} %param.19) | copy-start | bytes 30724
  8.6 17.5 %all-to-all-start = ((s32[32,1,8]{2,1,0:T(1,128)}), s32[32,1,8]{2,1,0:T(1,128)S(1)}, u32[]{:S(2)}, u32[]{:S(2)}) async-start(s32[32,1,8]{2,1,0:T(1,128)} %bitcast.92), calls=%async_computation | async-start | bytes 32768 | tf_op jit(solution)/shard_map/all_to_all | solution.py:190
  19.1 0.7 copy-start.8
  21.1 0.8 copy-start.3
  26.1 12.8 %all-to-all-start.2 = ((f32[32,8,6]{2,1,0:T(8,128)}), f32[32,8,6]{2,1,0:T(8,128)S(1)}, u32[]{:S(2)}, u32[]{:S(2)}) async-start(f32[32,8,6]{2,1,0:T(8,128)} %slice_bitcast_fusion.15), calls=%async_computation.2 | async-start | bytes 262144 | tf_op jit(solution)/shard_map/all_to_all | solution.py:192
  38.9 11.4 %all-to-all-start.1 = ((bf16[32,8,128]{2,1,0:T(8,128)(2,1)}), bf16[32,8,128]{2,1,0:T(8,128)(2,1)S(1)}, u32[]{:S(2)}, u32[]{:S(2)}) async-start(bf16[32,8,128]{2,1,0:T(8,128)(2,1)} %slice_bitcast_fusion.17), calls=%async_computation.1 | async-start | bytes 131072 | tf_op jit(solution)/shard_map/all_to_all | solution.py:189
  51.4 0.6 copy-start.1
  52.0 0.8 slice-start
  85.4 7.6 %copy-start = (bf16[2,2,128,1024]{3,2,1,0:T(8,128)(2,1)S(1)}, bf16[2,2,128,1024]{3,2,1,0:T(8,128)(2,1)}, u32[]{:S(2)}) copy-start(bf16[2,2,128,1024]{3,2,1,0:T(8,128)(2,1)} %param.21) | copy-start | bytes 3145732
  86.2 25.2 %all-to-all-start.3 = ((bf16[16,2,128,64]{2,3,1,0:T(8,128)(2,1)}), bf16[16,2,128,64]{2,3,1,0:T(8,128)(2,1)S(1)}, u32[]{:S(2)}, u32[]{:S(2)}) async-start(bf16[16,2,128,64]{2,3,1,0:T(8,128)(2,1)} %copy.118), calls=%async_computation.3 | async-start | bytes 1048576 | tf_op jit(solution)/shard_map/all_to_all | solution.py:28
  112.7 58.4 %all-to-all-start.5 = ((f32[16,2,128,64]{2,3,1,0:T(8,128)}), f32[16,2,128,64]{2,3,1,0:T(8,128)S(1)}, u32[]{:S(2)}, u32[]{:S(2)}) async-start(f32[16,2,128,64]{2,3,1,0:T(8,128)} %broadcast_in_dim.232), calls=%async_computation.5 | async-start | bytes 2097152 | tf_op jit(solution)/shard_map/all_to_all | solution.py:40
  171.1 15.5 %all-to-all-start.4 = ((s32[32,1,8]{2,1,0:T(1,128)}), s32[32,1,8]{2,1,0:T(1,128)S(1)}, u32[]{:S(2)}, u32[]{:S(2)}) async-start(s32[32,1,8]{2,1,0:T(1,128)} %bitcast.113), calls=%async_computation.4 | async-start | bytes 32768 | tf_op jit(solution)/shard_map/all_to_all | solution.py:190
  187.3 20.8 %all-to-all-start.6 = ((f32[16,1,2,1024]{3,2,1,0:T(2,128)}), f32[16,1,2,1024]{3,2,1,0:T(2,128)S(1)}, u32[]{:S(2)}, u32[]{:S(2)}) async-start(f32[16,1,2,1024]{3,2,1,0:T(2,128)} %broadcast_in_dim.233), calls=%async_computation.6 | async-start | bytes 262144 | tf_op jit(solution)/shard_map/all_to_all | solution.py:40
  219.9 15.0 %all-to-all-start.9 = ((f32[32,8,6]{2,1,0:T(8,128)}), f32[32,8,6]{2,1,0:T(8,128)S(1)}, u32[]{:S(2)}, u32[]{:S(2)}) async-start(f32[32,8,6]{2,1,0:T(8,128)} %bitcast_select_fusion.2), calls=%async_computation.9 | async-start | bytes 262144 | tf_op jit(solution)/shard_map/all_to_all | solution.py:244
  234.8 11.6 %all-to-all-start.7 = ((f32[32,8,128]{2,1,0:T(8,128)}), f32[32,8,128]{2,1,0:T(8,128)S(1)}, u32[]{:S(2)}, u32[]{:S(2)}) async-start(f32[32,8,128]{2,1,0:T(8,128)} %bitcast_select_fusion.3), calls=%async_computation.7 | async-start | bytes 262144 | tf_op jit(solution)/shard_map/all_to_all | solution.py:243
  246.5 11.6 %all-to-all-start.10 = ((f32[32,8,6]{2,1,0:T(8,128)}), f32[32,8,6]{2,1,0:T(8,128)S(1)}, u32[]{:S(2)}, u32[]{:S(2)}) async-start(f32[32,8,6]{2,1,0:T(8,128)} %slice_bitcast_fusion.14), calls=%async_computation.10 | async-start | bytes 262144 | tf_op jit(solution)/shard_map/all_to_all | solution.py:192
  258.1 11.4 %all-to-all-start.8 = ((bf16[32,8,128]{2,1,0:T(8,128)(2,1)}), bf16[32,8,128]{2,1,0:T(8,128)(2,1)S(1)}, u32[]{:S(2)}, u32[]{:S(2)}) async-start(bf16[32,8,128]{2,1,0:T(8,128)(2,1)} %slice_bitcast_fusion.16), calls=%async_computation.8 | async-start | bytes 131072 | tf_op jit(solution)/shard_map/all_to_all | solution.py:189
  270.6 0.6 copy-start.2
  271.3 0.8 slice-start.1
  300.3 22.5 %all-to-all-start.11 = ((bf16[16,2,128,64]{2,3,1,0:T(8,128)(2,1)}), bf16[16,2,128,64]{2,3,1,0:T(8,128)(2,1)S(1)}, u32[]{:S(2)}, u32[]{:S(2)}) async-start(bf16[16,2,128,64]{2,3,1,0:T(8,128)(2,1)} %copy.132), calls=%async_computation.11 | async-start | bytes 1048576 | tf_op jit(solution)/shard_map/all_to_all | solution.py:28
  324.0 58.5 %all-to-all-start.12 = ((f32[16,2,128,64]{2,3,1,0:T(8,128)}), f32[16,2,128,64]{2,3,1,0:T(8,128)S(1)}, u32[]{:S(2)}, u32[]{:S(2)}) async-start(f32[16,2,128,64]{2,3,1,0:T(8,128)} %broadcast_in_dim.239), calls=%async_computation.12 | async-start | bytes 2097152 | tf_op jit(solution)/shard_map/all_to_all | solution.py:40
  383.9 24.4 %all-to-all-start.13 = ((f32[16,1,2,1024]{3,2,1,0:T(2,128)}), f32[16,1,2,1024]{3,2,1,0:T(2,128)S(1)}, u32[]{:S(2)}, u32[]{:S(2)}) async-start(f32[16,1,2,1024]{3,2,1,0:T(2,128)} %broadcast_in_dim.240), calls=%async_computation.13 | async-start | bytes 262144 | tf_op jit(solution)/shard_map/all_to_all | solution.py:40
  419.9 15.0 %all-to-all-start.15 = ((f32[32,8,6]{2,1,0:T(8,128)}), f32[32,8,6]{2,1,0:T(8,128)S(1)}, u32[]{:S(2)}, u32[]{:S(2)}) async-start(f32[32,8,6]{2,1,0:T(8,128)} %bitcast_select_fusion), calls=%async_computation.15 | async-start | bytes 262144 | tf_op jit(solution)/shard_map/all_to_all | solution.py:244
  434.9 11.6 %all-to-all-start.14 = ((f32[32,8,128]{2,1,0:T(8,128)}), f32[32,8,128]{2,1,0:T(8,128)S(1)}, u32[]{:S(2)}, u32[]{:S(2)}) async-start(f32[32,8,128]{2,1,0:T(8,128)} %bitcast_select_fusion.1), calls=%async_computation.14 | async-start | bytes 262144 | tf_op jit(solution)/shard_map/all_to_all | solution.py:243
where the time goes:
time: 450 us; the launch traced here: 448 us
  waiting for transfers between devices  201 us (45%)
  starting transfers between devices  118 us (26%)
  blocking collectives  48.9 us (11%)
  local copies, waits for them, and re-layouts  37.7 us (8%)
  matrix products  21.2 us (5%)
  other arithmetic  18.5 us (4%)
    all_to_all x4, waiting for transfers between devices, from_everyone(): return lax.all_to_all(copies, axis, split_axis=0, concat_axis=0, tiled=True)  110 us
    all_gather x2, blocking collectives, body(): all_keeps = lax.all_gather(layer_keeps[None], 'depth', axis=0, tiled=True)  48.9 us
    all_to_all x4, starting transfers between devices, from_everyone(): return lax.all_to_all(copies, axis, split_axis=0, concat_axis=0, tiled=True)  48.4 us
    all_to_all x2, waiting for transfers between devices, sent_and_summed(): lax.all_to_all(tiles, axis, split_axis=0, concat_axis=0, tiled=True)  36.4 us
    all_to_all x2, starting transfers between devices, body(): lax.all_to_all(slot_buffer, 'tile', split_axis=0, concat_axis=0, tiled=True)  19 us
    dot_general x12, matrix products, block_sum(): jnp.einsum('ij,bjp->bip', triangle, blocks, precision=lax.Precision.HIGHEST)  15.4 us
    all_to_all x2, starting transfers between devices, body(): lax.all_to_all(back_shape, 'tile', split_axis=0, concat_axis=0, tiled=True)  14.5 us
    all_to_all x2, waiting for transfers between devices, body(): lax.all_to_all(back_shape, 'tile', split_axis=0, concat_axis=0, tiled=True)  12.5 us
  transfers between devices with their start and end apart: 16, of which 16 were waited for; matrix products, arithmetic and copies ran while one was open for 5% of the time, Pallas kernels for 0%

commit v1 on v0

v1 whole, which is shorter than its diff:
```python
import math
from functools import partial

import jax
import jax.numpy as jnp
from jax import lax
from jax.experimental import pallas as pl
from jax.experimental.pallas import tpu as pltpu
from jax.sharding import Mesh, PartitionSpec as P

F = 128
W = 32
S = 128
VIEWS = 2
P_SIZE = 1024
SHARE = 64
CAP = 8
ROWS = F + 8
GROUP = 1
UNROLL = 2
VMEM_LIMIT = 16 << 20

CLAMP = 0.99
RATE = 0.5
LOG2E = math.log2(math.e)

BF = jnp.bfloat16
F32 = jnp.float32
VMEM = pl.BlockSpec(memory_space=pltpu.VMEM)
SMEM = pl.BlockSpec(memory_space=pltpu.SMEM)


def dot(a, b, ca, cb):
    return lax.dot_general(a, b, (((ca,), (cb,)), ((), ())), preferred_element_type=F32)


def iota(shape, dim):
    return lax.broadcasted_iota(jnp.int32, shape, dim)


def split3(x):
    hi = x.astype(BF).astype(F32)
    rest = x - hi
    mid = rest.astype(BF).astype(F32)
    return hi, mid, rest - mid


def split2(x):
    hi = x.astype(BF)
    return hi, (x - hi.astype(F32)).astype(BF)


def joined3(x):
    return x[0:8] + (x[8:16] + x[16:24])


def stacked3(rows):
    hi, mid, lo = split3(rows)
    blank = jnp.zeros((F - 24, rows.shape[1]), F32)
    return jnp.concatenate([hi, mid, lo, blank], axis=0).astype(BF)


def strict(n, lower):
    i, j = iota((n, n), 0), iota((n, n), 1)
    return jnp.where(i > j if lower else i < j, 1.0, 0.0).astype(BF)


def routes(slots):
    owned = slots.shape[1]
    owners = owned // CAP
    visible = slots >= 0
    receiver = jnp.where(visible, slots >> (owned.bit_length() - 1), -1)
    to = jnp.where(receiver == iota((owners, owned), 0), 1.0, 0.0)
    rank = dot(to.astype(BF), strict(owned, False), 1, 0)
    place = jnp.sum(to * rank, axis=0, keepdims=True).astype(jnp.int32)
    position = jnp.where(visible, receiver * CAP + place, -1)
    return jnp.where(position == iota((owned, owned), 0), 1.0, 0.0).astype(BF)


def pack(feats, logits, slots, hot, row_ref, out_ref):
    owned = slots.shape[1]
    row_ref[5:6, :] = 1.0 / (1.0 + jnp.exp(-logits))
    row_ref[6:7, :] = ((slots & (owned - 1)) + 1).astype(F32)
    rows = dot(hot, feats, 1, 0).astype(BF)
    extra = dot(hot, stacked3(row_ref[...]), 1, 1).astype(BF)
    for copy in range(out_ref.shape[0] // owned):
        out_ref[copy * owned : (copy + 1) * owned, 0:F] = rows
        out_ref[copy * owned : (copy + 1) * owned, F : 2 * F] = extra


def route_kernel(slots_ref, hot_ref, *, view):
    hot_ref[...] = routes(slots_ref[view])


def geometry_rows(geometry_ref, row_ref, view):
    row_ref[...] = jnp.zeros_like(row_ref)
    for k in range(5):
        row_ref[k : k + 1, :] = geometry_ref[view * 5 + k]


def pack_kernel(feats_ref, logits_ref, geometry_ref, slots_ref, out_ref, hot_ref, row_ref):
    slots = slots_ref[0]
    hot = routes(slots)
    hot_ref[...] = hot
    geometry_rows(geometry_ref, row_ref, 0)
    pack(feats_ref[...], logits_ref[...], slots, hot, row_ref, out_ref)


def update(ret_ref, feats_ref, logits_ref, hot):
    owned = hot.shape[0]
    total = jnp.zeros((owned, F), F32)
    extra = jnp.zeros((8, owned), F32)
    for copy in range(ret_ref.shape[0] // owned):
        block = slice(copy * owned, (copy + 1) * owned)
        total += dot(hot, ret_ref[block, 0:F], 0, 0)
        total += dot(hot, ret_ref[block, F : 2 * F], 0, 0)
        extra += joined3(dot(ret_ref[block, 2 * F : 3 * F], hot, 0, 0))
    feats = (feats_ref[...].astype(F32) - RATE * total).astype(BF)
    logits = logits_ref[...] - RATE * extra[5:6]
    return feats, logits, extra


def update_pack_kernel(
    ret_ref,
    feats_ref,
    logits_ref,
    slots_ref,
    geometry_ref,
    hot_ref,
    next_ref,
    out_ref,
    new_feats_ref,
    new_logits_ref,
    grads_ref,
    row_ref,
    *,
    view,
):
    feats, logits, extra = update(ret_ref, feats_ref, logits_ref, hot_ref[...])
    grads_ref[...] = extra
    new_feats_ref[...] = feats
    new_logits_ref[...] = logits
    geometry_rows(geometry_ref, row_ref, view)
    pack(feats, logits, slots_ref[view], next_ref[...], row_ref, out_ref)


def update_kernel(
    ret_ref,
    feats_ref,
    logits_ref,
    hot_ref,
    *refs,
):
    *earlier, new_feats_ref, new_logits_ref, grads_ref = refs
    feats, logits, extra = update(ret_ref, feats_ref, logits_ref, hot_ref[...])
    new_feats_ref[...] = feats
    new_logits_ref[...] = logits
    for v, rows in enumerate([ref[...] for ref in earlier] + [extra]):
        for k in range(5):
            grads_ref[v * 5 + k] = rows[k : k + 1]


def landing(got_ref, layer, owned):
    block = slice(layer * owned, (layer + 1) * owned)
    slot = got_ref[block, F : 2 * F].astype(F32)[:, 6:7]
    lane = (iota((owned, owned), 1) + 1).astype(F32)
    return jnp.where(slot == lane, 1.0, 0.0).astype(BF)


def columns(shapes_ref, tile, width):
    cols = slice(tile * width, (tile + 1) * width)
    g0 = shapes_ref[0:1, cols]
    g2, g3 = shapes_ref[2:3, cols], shapes_ref[3:4, cols]
    coef_a, coef_c = jnp.exp(g2), jnp.exp(g3)
    spread = jnp.exp(0.5 * (g2 + g3))
    coef_b = shapes_ref[4:5, cols] * spread
    delta_x = iota((W, width), 0).astype(F32) + 0.5 - g0
    return coef_a, coef_b, coef_c, spread, delta_x


def x_terms(shapes_ref, x_ref, width):
    for tile in range(2):
        coef_a, coef_b, coef_c, _, delta_x = columns(shapes_ref, tile, width)
        x_ref[0, tile] = (-0.5 * LOG2E) * coef_a * delta_x * delta_x
        x_ref[1, tile] = (-LOG2E) * coef_b * delta_x
        x_ref[2, tile] = delta_x
        x_ref[3, tile, 0:1] = (-0.5 * LOG2E) * coef_c


def products(shapes_ref, x_ref, top, width):
    parts = []
    for tile in range(2):
        cols = slice(tile * width, (tile + 1) * width)
        for line in range(SHARE // W):
            delta_y = (top + (line + 0.5)) - shapes_ref[1:2, cols]
            level = x_ref[3, tile, 0:1] * delta_y * delta_y
            power = x_ref[0, tile] + (x_ref[1, tile] * delta_y + level)
            parts.append(jnp.exp2(power) * shapes_ref[5:6, cols])
    return jnp.concatenate(parts, axis=0)


def apart(weights, width):
    half = weights.shape[0] // 2
    blank = jnp.zeros((half, width), BF)
    return jnp.concatenate(
        [
            jnp.concatenate([weights[:half], blank], axis=1),
            jnp.concatenate([blank, weights[half:]], axis=1),
        ],
        axis=0,
    )


def parts_rows(rows):
    hi, mid, lo = split3(rows)
    k = iota(rows.shape, 0)
    return jnp.where(
        k == 0, hi, jnp.where(k == 1, mid, jnp.where(k == 2, lo, 0.0))
    ).astype(BF)


def share_top(pos_ref, chunk, group):
    return ((SHARE // W) * (chunk * group + pos_ref[0])).astype(F32)


def forward_kernel(
    pos_ref, got_ref, out_ref, feats_ref, shapes_ref, hot_ref, x_ref, tri_ref
):
    owned = 2 * S
    group = got_ref.shape[0] // owned
    width = S * group
    for layer in range(group):
        block = slice(layer * owned, (layer + 1) * owned)
        hot = landing(got_ref, layer, owned)
        hot_ref[block, :] = hot
        feats = dot(got_ref[block, 0:F], hot, 0, 0).astype(BF)
        shapes = joined3(dot(got_ref[block, F : 2 * F], hot, 0, 0))
        for tile in range(2):
            at = slice(tile * width + layer * S, tile * width + (layer + 1) * S)
            feats_ref[:, at] = feats[:, tile * S : (tile + 1) * S]
            shapes_ref[:, at] = shapes[:, tile * S : (tile + 1) * S]
    x_terms(shapes_ref, x_ref, width)
    tri_ref[0:width, :] = strict(width, False)
    tri_ref[width : 2 * width, :] = tri_ref[0:width, :]
    ones = jnp.ones((8, 2 * width), BF)

    def step(chunk, carry):
        product = products(shapes_ref, x_ref, share_top(pos_ref, chunk, group), width)
        coverage = jnp.minimum(product, CLAMP)
        pieces = jnp.concatenate(split2(jnp.log(1.0 - coverage)), axis=1)
        before = dot(pieces, tri_ref[...], 1, 0)
        weights = (coverage * jnp.exp(before)).astype(BF)
        out_ref[chunk, 0:F, :] = dot(feats_ref[...], apart(weights, width), 1, 1).astype(BF)
        out_ref[chunk, F:ROWS, :] = parts_rows(jnp.exp(dot(ones, pieces, 1, 1)))
        return carry

    lax.fori_loop(0, out_ref.shape[0], step, 0, unroll=UNROLL)


def prepare_kernel(pos_ref, shapes_ref, exact_ref, odds_ref, x_ref, tri_ref):
    width = exact_ref.shape[2]
    group = width // S
    x_terms(shapes_ref, x_ref, width)
    tri_ref[0:width, :] = strict(width, False)
    tri_ref[width : 2 * width, :] = tri_ref[0:width, :]

    def step(chunk, carry):
        product = products(shapes_ref, x_ref, share_top(pos_ref, chunk, group), width)
        coverage = jnp.minimum(product, CLAMP)
        left = 1.0 - coverage
        before = dot(jnp.concatenate(split2(jnp.log(left)), axis=1), tri_ref[...], 1, 0)
        exact_ref[chunk] = coverage * jnp.exp(before)
        odds_ref[chunk] = jnp.where(product < CLAMP, product / left, 0.0)
        return carry

    lax.fori_loop(0, exact_ref.shape[0], step, 0, unroll=UNROLL)


def pixel_kernel(got_ref, target_ref, image_ref, out_ref):
    groups = got_ref.shape[0]
    summed = jnp.zeros((F, 2 * SHARE), F32)
    ahead = jnp.ones((1, 2 * SHARE), F32)
    aheads, keeps = [], []
    for d in range(groups):
        rows = got_ref[d, F:ROWS, :].astype(F32)
        keep = rows[0:1] + (rows[1:2] + rows[2:3])
        summed += ahead * got_ref[d, 0:F, :].astype(F32)
        aheads.append(ahead)
        keeps.append(keep)
        ahead = ahead * keep
    image_ref[...] = summed.T.astype(BF)
    residual = summed - target_ref[...].astype(F32)
    behind = jnp.zeros((1, 2 * SHARE), F32)
    for d in reversed(range(groups)):
        carry = aheads[d] * behind * keeps[d]
        out_ref[d, 0:F, :] = (aheads[d] * residual).astype(BF)
        out_ref[d, F:ROWS, :] = parts_rows(jnp.broadcast_to(carry, (8, 2 * SHARE)))
        if d:
            term = jnp.sum(residual * got_ref[d, 0:F, :].astype(F32), axis=0, keepdims=True)
            behind = term + keeps[d] * behind


def folded(x):
    total = x[0:8]
    for k in range(8, x.shape[0], 8):
        total = total + x[k : k + 8]
    return total


def backward_kernel(
    pos_ref,
    hot_ref,
    feats_ref,
    shapes_ref,
    exact_ref,
    odds_ref,
    grad_ref,
    out_ref,
    x_ref,
    tri_ref,
    sum_ref,
    acc_ref,
):
    owned = 2 * S
    group = hot_ref.shape[0] // owned
    width = S * group
    for tile in range(2):
        x_ref[tile] = columns(shapes_ref, tile, width)[4]
    tri_ref[0:width, :] = strict(width, True)
    tri_ref[width : 2 * width, :] = tri_ref[0:width, :]
    sum_ref[...] = jnp.zeros_like(sum_ref)
    acc_ref[...] = jnp.zeros_like(acc_ref)
    ones = jnp.ones((8, width), BF)

    def step(chunk, carry):
        exact = exact_ref[chunk]
        odds = odds_ref[chunk]
        grad = grad_ref[chunk, 0:F, :]
        both = dot(grad, feats_ref[...], 0, 0)
        grad_weight = jnp.concatenate(
            [both[0:SHARE, 0:width], both[SHARE : 2 * SHARE, width : 2 * width]], axis=0
        )
        grad_before = grad_weight * exact
        later = dot(jnp.concatenate(split2(grad_before), axis=1), tri_ref[...], 1, 0)
        grad_log = later + dot(grad_ref[chunk, F:ROWS, :], ones, 0, 0)
        acc_ref[...] += dot(grad, apart(exact.astype(BF), width), 1, 0)
        scaled = jnp.where(odds > 0.0, grad_before, 0.0) - grad_log * odds
        top = share_top(pos_ref, chunk, group)
        for tile in range(2):
            delta_x = x_ref[tile]
            g1 = shapes_ref[1:2, tile * width : (tile + 1) * width]
            for line in range(SHARE // W):
                k = tile * (SHARE // W) + line
                delta_y = (top + (line + 0.5)) - g1
                row = scaled[k * W : (k + 1) * W]
                row_x = row * delta_x
                sum_0, sum_x, sum_xx = folded(row), folded(row_x), folded(row_x * delta_x)
                sum_y = sum_0 * delta_y
                sum_ref[tile, 0] += sum_0
                sum_ref[tile, 1] += sum_x
                sum_ref[tile, 2] += sum_y
                sum_ref[tile, 3] += sum_xx
                sum_ref[tile, 4] += sum_x * delta_y
                sum_ref[tile, 5] += sum_y * delta_y
        return carry

    lax.fori_loop(0, grad_ref.shape[0], step, 0, unroll=UNROLL)
    for tile in range(2):
        cols = slice(tile * width, (tile + 1) * width)
        coef_a, coef_b, coef_c, spread, _ = columns(shapes_ref, tile, width)
        total = [jnp.sum(sum_ref[tile, k], axis=0, keepdims=True) for k in range(6)]
        first, cross, second = -0.5 * total[3], -total[4], -0.5 * total[5]
        sum_ref[tile, 0, 0:1] = coef_a * total[1] + coef_b * total[2]
        sum_ref[tile, 0, 1:2] = coef_b * total[1] + coef_c * total[2]
        sum_ref[tile, 0, 2:3] = coef_a * first + 0.5 * coef_b * cross
        sum_ref[tile, 0, 3:4] = coef_c * second + 0.5 * coef_b * cross
        sum_ref[tile, 0, 4:5] = spread * cross
        sum_ref[tile, 0, 5:6] = (1.0 - shapes_ref[5:6, cols]) * total[0]
        sum_ref[tile, 0, 6:8] = jnp.zeros((2, width), F32)
    for layer in range(group):
        block = slice(layer * owned, (layer + 1) * owned)
        hot = hot_ref[block, :]
        feat = jnp.concatenate(
            [acc_ref[:, t * width + layer * S : t * width + (layer + 1) * S] for t in range(2)],
            axis=1,
        )
        rows = jnp.concatenate(
            [sum_ref[t, 0, :, layer * S : (layer + 1) * S] for t in range(2)], axis=1
        )
        hi, lo = split2(feat)
        out_ref[block, 0:F] = dot(hot, hi, 1, 1).astype(BF)
        out_ref[block, F : 2 * F] = dot(hot, lo, 1, 1).astype(BF)
        out_ref[block, 2 * F : 3 * F] = dot(hot, stacked3(rows), 1, 1).astype(BF)


def call(kernel, outs, ins, scratch=(), name=None, cost=None):
    specs = [SMEM if x.dtype == jnp.int32 and x.shape == (1,) else VMEM for x in ins]
    return pl.pallas_call(
        kernel,
        out_shape=tuple(jax.ShapeDtypeStruct(shape, dtype) for shape, dtype in outs),
        in_specs=specs,
        out_specs=tuple(VMEM for _ in outs),
        scratch_shapes=list(scratch),
        compiler_params=pltpu.CompilerParams(vmem_limit_bytes=VMEM_LIMIT),
        cost_estimate=cost,
        name=name,
    )(*ins)


def exchanged(x, axis, size):
    blocks = x.reshape(size, x.shape[0] // size, *x.shape[1:])
    return lax.all_to_all(blocks, axis, split_axis=0, concat_axis=0, tiled=True).reshape(x.shape)


def body(features, logits, geometry, dest_slot, target):
    owners = lax.axis_size("tile")
    group = lax.axis_size("low")
    groups = lax.axis_size("high")
    low = lax.axis_index("low")
    depth_here = lax.axis_index("high") * group + low
    owned = features.shape[1]
    width = S * group
    pos = low.astype(jnp.int32).reshape(1)
    around = ("low", "tile") if group > 1 else "tile"
    feats, now = features[0], logits
    slots = dest_slot
    geometry = geometry.transpose(0, 2, 1, 3).reshape(VIEWS * 5, 1, owned)
    targets = [
        lax.dynamic_slice_in_dim(target[v], depth_here * SHARE, SHARE, 2)
        .transpose(1, 0, 2)
        .reshape(F, 2 * SHARE)
        for v in range(VIEWS)
    ]
    send_shape = ((group * owned, 2 * F), BF)
    hot_shape = ((owned, owned), BF)
    row_scratch = pltpu.VMEM((8, owned), F32)
    x_scratch = pltpu.VMEM((4, 2, W, width), F32)
    tri_scratch = pltpu.VMEM((2 * width, width), BF)
    plane = ((groups, 2 * SHARE, width), F32)
    send, hot = call(
        pack_kernel,
        [send_shape, hot_shape],
        [feats, now, geometry, slots],
        [row_scratch],
        "pack",
    )
    images, shape_grads = [], []
    for v in range(VIEWS):
        got = exchanged(send, around, group * owners)
        composites, slot_feats, slot_shapes, landed = call(
            forward_kernel,
            [
                ((groups, ROWS, 2 * SHARE), BF),
                ((F, 2 * width), BF),
                ((8, 2 * width), F32),
                ((group * owned, owned), BF),
            ],
            [pos, got],
            [x_scratch, tri_scratch],
            "forward",
        )
        arrived = exchanged(composites, "high", groups)
        exact, odds = call(
            prepare_kernel,
            [plane, plane],
            [pos, slot_shapes],
            [x_scratch, tri_scratch],
            "prepare",
        )
        image, grad_comp = call(
            pixel_kernel,
            [((2 * SHARE, F), BF), ((groups, ROWS, 2 * SHARE), BF)],
            [arrived, targets[v]],
            name="pixels",
        )
        images.append(image.reshape(2, SHARE, F))
        grads = exchanged(grad_comp, "high", groups)
        (back,) = call(
            backward_kernel,
            [((group * owned, 3 * F), BF)],
            [pos, landed, slot_feats, slot_shapes, exact, odds, grads],
            [
                pltpu.VMEM((2, W, width), F32),
                tri_scratch,
                pltpu.VMEM((2, 6, 8, width), F32),
                pltpu.VMEM((F, 2 * width), F32),
            ],
            "backward",
        )
        ret = exchanged(back, around, group * owners)
        state = [((owned, F), BF), ((1, owned), F32)]
        if v + 1 < VIEWS:
            (next_hot,) = call(
                partial(route_kernel, view=v + 1), [hot_shape], [slots], name="route"
            )
            send, feats, now, shape_grad = call(
                partial(update_pack_kernel, view=v + 1),
                [send_shape, *state, ((8, owned), F32)],
                [ret, feats, now, slots, geometry, hot, next_hot],
                [row_scratch],
                "update_pack",
            )
            shape_grads.append(shape_grad)
            hot = next_hot
        else:
            feats, now, grads = call(
                update_kernel,
                [*state, ((VIEWS * 5, 1, owned), F32)],
                [ret, feats, now, hot, *shape_grads],
                name="update",
            )
    grads = grads.reshape(VIEWS, 5, 1, owned).transpose(0, 2, 1, 3)
    return (jnp.stack(images).transpose(0, 1, 3, 2), feats[None], now, grads)


def solution(mesh):
    tiles, layers = mesh.devices.shape
    split = Mesh(
        mesh.devices.reshape(tiles, layers // GROUP, GROUP), ("tile", "high", "low")
    )
    depth = ("high", "low")
    return jax.shard_map(
        body,
        mesh=split,
        in_specs=(
            P(depth, "tile", None),
            P(depth, "tile"),
            P(None, depth, None, "tile"),
            P(None, depth, "tile"),
            P(None, "tile", None, None),
        ),
        out_specs=(
            P(None, "tile", None, depth),
            P(depth, "tile", None),
            P(depth, "tile"),
            P(None, depth, None, "tile"),
        ),
        check_vma=False,
    )
```

time: 450 us -> 235 us (0.52)
  waiting for transfers between devices: 201 us -> 107 us
  starting transfers between devices: 118 us -> 67.1 us
  local copies, waits for them, and re-layouts: 37.7 us -> 2.85 us
  Pallas kernels: 0 us -> 26.9 us
  matrix products: 21.2 us -> 0 us
  blocking collectives: 48.9 us -> 28.4 us
  other arithmetic: 18.5 us -> 0.64 us
    all_to_all x16 -> x6, waiting for transfers between devices: 201 us -> 107 us  [exchanged(): lax.all_to_all(blocks, axis, split_axis=0, concat_axis=0, tiled=True)]
    all_to_all x16 -> x6, starting transfers between devices: 118 us -> 67.1 us  [exchanged(): lax.all_to_all(blocks, axis, split_axis=0, concat_axis=0, tiled=True)]
    all_gather x2 -> x0, blocking collectives: 48.9 us -> none  [body(): all_keeps = lax.all_gather(layer_keeps[None], 'depth', axis=0, tiled=True)]
    all_to_all x0 -> x2, blocking collectives: none -> 28.4 us  [exchanged(): lax.all_to_all(blocks, axis, split_axis=0, concat_axis=0, tiled=True)]
    pallas_call x0 -> x12, Pallas kernels: none -> 26.9 us  [call(): pl.pallas_call(kernel, out_shape=tuple((jax.ShapeDtypeStruct(shape, dtype...]
    dot_general x24 -> x0, matrix products: 21.2 us -> none  [the longest x12 15.4 us: block_sum(): jnp.einsum('ij,bjp->bip', triangle, blocks, precision=lax.Precision.HIGHEST)]
    scatter x9 -> x0, local copies, waits for them, and re-layouts: 11 us -> none  [the longest x2 2.79 us: body(): slot_buffer = jnp.full((owners * capacity + 1,), -1, jnp.int32).at[positi...]
    reduce_sum x18 -> x0, other arithmetic: 7.33 us -> none  [the longest x8 4.04 us: block_sum(): block_totals = jnp.sum(blocks, axis=1)]
  transfers between devices with their start and end apart: 16 -> 6, of which waited for: 16 -> 6; matrix products, arithmetic and copies ran while one was open for 5% -> 1% of each run, Pallas kernels for 0% -> 2%
where the time goes in v1:
time: 235 us; the launch traced here: 234 us
  waiting for transfers between devices  107 us (46%)
  starting transfers between devices  67.1 us (29%)
  blocking collectives  28.4 us (12%)
  Pallas kernels  26.9 us (11%)
  local copies, waits for them, and re-layouts  2.85 us (1%)
    all_to_all x6, waiting for transfers between devices, exchanged(): lax.all_to_all(blocks, axis, split_axis=0, concat_axis=0, tiled=True)  107 us
    all_to_all x6, starting transfers between devices, exchanged(): lax.all_to_all(blocks, axis, split_axis=0, concat_axis=0, tiled=True)  67.1 us
    all_to_all x2, blocking collectives, exchanged(): lax.all_to_all(blocks, axis, split_axis=0, concat_axis=0, tiled=True)  28.4 us
    pallas_call x12, Pallas kernels, call(): pl.pallas_call(kernel, out_shape=tuple((jax.ShapeDtypeStruct(shape, dtype...  26.9 us
  transfers between devices with their start and end apart: 6, of which 6 were waited for; matrix products, arithmetic and copies ran while one was open for 1% of the time, Pallas kernels for 2%

profile of v1, /device:TPU:1, one launch (start us, length us, event | category | flops | bytes accessed | tf_op | source)
XLA Modules:
  0.0 233.8 jit_solution(15343630997711232794)
XLA Ops:
  0.7 0.7 copy-done.4
  1.3 0.8 copy-done
  2.2 0.7 copy-done.2
  2.9 0.4 pack.1
  3.3 17.2 %all_to_all.40 = bf16[32,8,256]{2,1,0:T(8,128)(2,1)S(1)} all-to-all(bf16[32,8,256]{2,1,0:T(8,128)(2,1)S(1)} %bitcast.53), channel_id=1, replica_groups=mesh['tile'=32,'depth'=16] {'tile'}, dimensions={0} | all-to-all | bytes 262144 | tf_op jit(solution)/shard_map/all_to_all | solution.py:412
  20.4 4.3 %forward.2 = (bf16[16,136,128]{2,1,0:T(8,128)(2,1)}, bf16[128,256]{1,0:T(8,128)(2,1)S(1)}, f32[8,256]{1,0:T(8,128)S(1)}, bf16[256,256]{1,0:T(8,128)(2,1)S(1)}) custom-call(s32[1]{0:T(128)} %constant.11.clone.1.pos_ref, bf16[256,256]{1,0:T(8,128)(2,1)S(1)} %bitcast.48), custom_call_target="tpu_custom_call" | custom-call | tf_op jit(solution)/shard_map/forward/pallas_call | solution.py:398
  24.7 13.7 %all-to-all-start.1 = ((bf16[16,1,136,128]{3,2,1,0:T(8,128)(2,1)}), bf16[16,1,136,128]{3,2,1,0:T(8,128)(2,1)S(1)}, u32[]{:S(2)}, u32[]{:S(2)}) async-start(bf16[16,1,136,128]{3,2,1,0:T(8,128)(2,1)} %bitcast.5), calls=%async_computation.1 | async-start | bytes 1114112 | tf_op jit(solution)/shard_map/all_to_all | solution.py:412
  38.8 0.1 copy.15.target_ref
  38.9 23.4 %all-to-all-done.1 = bf16[16,1,136,128]{3,2,1,0:T(8,128)(2,1)S(1)} async-done(((bf16[16,1,136,128]{3,2,1,0:T(8,128)(2,1)}), bf16[16,1,136,128]{3,2,1,0:T(8,128)(2,1)S(1)}, u32[]{:S(2)}, u32[]{:S(2)}) %all-to-all-start.1) | async-done | bytes 557088 | tf_op jit(solution)/shard_map/all_to_all | solution.py:412
  62.3 1.2 pixels.2
  63.5 13.1 %all-to-all-start.2 = ((bf16[16,1,136,128]{3,2,1,0:T(8,128)(2,1)}), bf16[16,1,136,128]{3,2,1,0:T(8,128)(2,1)S(1)}, u32[]{:S(2)}, u32[]{:S(2)}) async-start(bf16[16,1,136,128]{3,2,1,0:T(8,128)(2,1)} %bitcast.12), calls=%async_computation.2 | async-start | bytes 1114112 | tf_op jit(solution)/shard_map/all_to_all | solution.py:412
  76.6 1.9 prepare.2
  78.5 22.1 %all-to-all-done.2 = bf16[16,1,136,128]{3,2,1,0:T(8,128)(2,1)S(1)} async-done(((bf16[16,1,136,128]{3,2,1,0:T(8,128)(2,1)}), bf16[16,1,136,128]{3,2,1,0:T(8,128)(2,1)S(1)}, u32[]{:S(2)}, u32[]{:S(2)}) %all-to-all-start.2) | async-done | bytes 557088 | tf_op jit(solution)/shard_map/all_to_all | solution.py:412
  100.6 5.1 %backward.2 = bf16[256,384]{1,0:T(8,128)(2,1)} custom-call(s32[1]{0:T(128)} %constant.11.clone.1.pos_ref, bf16[256,256]{1,0:T(8,128)(2,1)S(1)} %get-tuple-element.32.hot_ref, bf16[128,256]{1,0:T(8,128)(2,1)S(1)} %get-tuple-element.33.feats_ref, f32[8,256]{1,0:T(8,128)S(1)} %get-tuple-element.34.shapes_ref, f32[16,128,128]{2,1,0:T(8,128)S(1)} %get-tuple-element.35.exact_ref, ...), custom_call_target="tpu_custom_call" | custom-call | tf_op jit(solution)/shard_map/backward/pallas_call | solution.py:398
  105.7 10.2 %all-to-all-start.3 = ((bf16[32,8,384]{2,1,0:T(8,128)(2,1)}), bf16[32,8,384]{2,1,0:T(8,128)(2,1)S(1)}, u32[]{:S(2)}, u32[]{:S(2)}) async-start(bf16[32,8,384]{2,1,0:T(8,128)(2,1)} %bitcast.14), calls=%async_computation.3 | async-start | bytes 393216 | tf_op jit(solution)/shard_map/all_to_all | solution.py:412
  116.0 0.2 route.1.next_ref.hot_ref
  116.2 8.1 %all-to-all-done.3 = bf16[32,8,384]{2,1,0:T(8,128)(2,1)S(1)} async-done(((bf16[32,8,384]{2,1,0:T(8,128)(2,1)}), bf16[32,8,384]{2,1,0:T(8,128)(2,1)S(1)}, u32[]{:S(2)}, u32[]{:S(2)}) %all-to-all-start.3) | async-done | bytes 196640 | tf_op jit(solution)/shard_map/all_to_all | solution.py:412
  124.3 0.5 update_pack.1
  124.8 11.2 %all_to_all.41 = bf16[32,8,256]{2,1,0:T(8,128)(2,1)S(1)} all-to-all(bf16[32,8,256]{2,1,0:T(8,128)(2,1)S(1)} %bitcast.52), channel_id=1, replica_groups=mesh['tile'=32,'depth'=16] {'tile'}, dimensions={0} | all-to-all | bytes 262144 | tf_op jit(solution)/shard_map/all_to_all | solution.py:412
  136.0 4.3 %forward.3 = (bf16[16,136,128]{2,1,0:T(8,128)(2,1)}, bf16[128,256]{1,0:T(8,128)(2,1)S(1)}, f32[8,256]{1,0:T(8,128)S(1)}, bf16[256,256]{1,0:T(8,128)(2,1)S(1)}) custom-call(s32[1]{0:T(128)} %constant.11.clone.1.pos_ref, bf16[256,256]{1,0:T(8,128)(2,1)S(1)} %bitcast.49), custom_call_target="tpu_custom_call" | custom-call | tf_op jit(solution)/shard_map/forward/pallas_call | solution.py:398
  140.3 6.7 %all-to-all-start.5 = ((bf16[16,1,136,128]{3,2,1,0:T(8,128)(2,1)}), bf16[16,1,136,128]{3,2,1,0:T(8,128)(2,1)S(1)}, u32[]{:S(2)}, u32[]{:S(2)}) async-start(bf16[16,1,136,128]{3,2,1,0:T(8,128)(2,1)} %bitcast.19), calls=%async_computation.5 | async-start | bytes 1114112 | tf_op jit(solution)/shard_map/all_to_all | solution.py:412
  147.1 0.1 copy.19.target_ref
  147.2 23.6 %all-to-all-done.5 = bf16[16,1,136,128]{3,2,1,0:T(8,128)(2,1)S(1)} async-done(((bf16[16,1,136,128]{3,2,1,0:T(8,128)(2,1)}), bf16[16,1,136,128]{3,2,1,0:T(8,128)(2,1)S(1)}, u32[]{:S(2)}, u32[]{:S(2)}) %all-to-all-start.5) | async-done | bytes 557088 | tf_op jit(solution)/shard_map/all_to_all | solution.py:412
  170.8 1.2 pixels.3
  172.0 13.1 %all-to-all-start.6 = ((bf16[16,1,136,128]{3,2,1,0:T(8,128)(2,1)}), bf16[16,1,136,128]{3,2,1,0:T(8,128)(2,1)S(1)}, u32[]{:S(2)}, u32[]{:S(2)}) async-start(bf16[16,1,136,128]{3,2,1,0:T(8,128)(2,1)} %bitcast.27), calls=%async_computation.6 | async-start | bytes 1114112 | tf_op jit(solution)/shard_map/all_to_all | solution.py:412
  185.1 1.9 prepare.3
  187.0 22.1 %all-to-all-done.6 = bf16[16,1,136,128]{3,2,1,0:T(8,128)(2,1)S(1)} async-done(((bf16[16,1,136,128]{3,2,1,0:T(8,128)(2,1)}), bf16[16,1,136,128]{3,2,1,0:T(8,128)(2,1)S(1)}, u32[]{:S(2)}, u32[]{:S(2)}) %all-to-all-start.6) | async-done | bytes 557088 | tf_op jit(solution)/shard_map/all_to_all | solution.py:412
  209.2 5.1 %backward.3 = bf16[256,384]{1,0:T(8,128)(2,1)} custom-call(s32[1]{0:T(128)} %constant.11.clone.1.pos_ref, bf16[256,256]{1,0:T(8,128)(2,1)S(1)} %get-tuple-element.42.hot_ref, bf16[128,256]{1,0:T(8,128)(2,1)S(1)} %get-tuple-element.43.feats_ref, f32[8,256]{1,0:T(8,128)S(1)} %get-tuple-element.44.shapes_ref, f32[16,128,128]{2,1,0:T(8,128)S(1)} %get-tuple-element.45.exact_ref, ...), custom_call_target="tpu_custom_call" | custom-call | tf_op jit(solution)/shard_map/backward/pallas_call | solution.py:398
  214.2 10.3 %all-to-all-start.7 = ((bf16[32,8,384]{2,1,0:T(8,128)(2,1)}), bf16[32,8,384]{2,1,0:T(8,128)(2,1)S(1)}, u32[]{:S(2)}, u32[]{:S(2)}) async-start(bf16[32,8,384]{2,1,0:T(8,128)(2,1)} %bitcast.29), calls=%async_computation.7 | async-start | bytes 393216 | tf_op jit(solution)/shard_map/all_to_all | solution.py:412
  224.5 0.6 maximum_bitcast_fusion
  225.1 7.7 %all-to-all-done.7 = bf16[32,8,384]{2,1,0:T(8,128)(2,1)S(1)} async-done(((bf16[32,8,384]{2,1,0:T(8,128)(2,1)}), bf16[32,8,384]{2,1,0:T(8,128)(2,1)S(1)}, u32[]{:S(2)}, u32[]{:S(2)}) %all-to-all-start.7) | async-done | bytes 196640 | tf_op jit(solution)/shard_map/all_to_all | solution.py:412
  232.8 0.9 update.1
  (15 shorter events, 0.4 us)
Async XLA Ops:
  0.6 0.7 copy-start.4
  0.6 0.7 copy-start.5
  1.3 0.8 copy-start
  2.2 0.7 copy-start.2
  2.9 35.6 %copy-start.6 = (bf16[2,2,128,1024]{3,2,1,0:T(8,128)(2,1)S(1)}, bf16[2,2,128,1024]{3,2,1,0:T(8,128)(2,1)}, u32[]{:S(2)}) copy-start(bf16[2,2,128,1024]{3,2,1,0:T(8,128)(2,1)} %param.9) | copy-start | bytes 3145732
  24.7 37.6 %all-to-all-start.1 = ((bf16[16,1,136,128]{3,2,1,0:T(8,128)(2,1)}), bf16[16,1,136,128]{3,2,1,0:T(8,128)(2,1)S(1)}, u32[]{:S(2)}, u32[]{:S(2)}) async-start(bf16[16,1,136,128]{3,2,1,0:T(8,128)(2,1)} %bitcast.5), calls=%async_computation.1 | async-start | bytes 1114112 | tf_op jit(solution)/shard_map/all_to_all | solution.py:412
  63.5 37.2 %all-to-all-start.2 = ((bf16[16,1,136,128]{3,2,1,0:T(8,128)(2,1)}), bf16[16,1,136,128]{3,2,1,0:T(8,128)(2,1)S(1)}, u32[]{:S(2)}, u32[]{:S(2)}) async-start(bf16[16,1,136,128]{3,2,1,0:T(8,128)(2,1)} %bitcast.12), calls=%async_computation.2 | async-start | bytes 1114112 | tf_op jit(solution)/shard_map/all_to_all | solution.py:412
  105.7 18.6 %all-to-all-start.3 = ((bf16[32,8,384]{2,1,0:T(8,128)(2,1)}), bf16[32,8,384]{2,1,0:T(8,128)(2,1)S(1)}, u32[]{:S(2)}, u32[]{:S(2)}) async-start(bf16[32,8,384]{2,1,0:T(8,128)(2,1)} %bitcast.14), calls=%async_computation.3 | async-start | bytes 393216 | tf_op jit(solution)/shard_map/all_to_all | solution.py:412
  116.0 8.4 %copy-start.1 = (bf16[1,256,128]{2,1,0:T(8,128)(2,1)S(1)}, bf16[1,256,128]{2,1,0:T(8,128)(2,1)}, u32[]{:S(2)}) copy-start(bf16[1,256,128]{2,1,0:T(8,128)(2,1)} %param.5) | copy-start | bytes 196612
  116.0 8.3 %copy-start.3 = (f32[2,1,5,256]{3,1,2,0:T(1,128)S(1)}, f32[2,1,5,256]{3,1,2,0:T(1,128)}, u32[]{:S(2)}) copy-start(f32[2,1,5,256]{3,1,2,0:T(1,128)} %param.7) | copy-start | bytes 30724
  140.3 30.6 %all-to-all-start.5 = ((bf16[16,1,136,128]{3,2,1,0:T(8,128)(2,1)}), bf16[16,1,136,128]{3,2,1,0:T(8,128)(2,1)S(1)}, u32[]{:S(2)}, u32[]{:S(2)}) async-start(bf16[16,1,136,128]{3,2,1,0:T(8,128)(2,1)} %bitcast.19), calls=%async_computation.5 | async-start | bytes 1114112 | tf_op jit(solution)/shard_map/all_to_all | solution.py:412
  172.0 37.2 %all-to-all-start.6 = ((bf16[16,1,136,128]{3,2,1,0:T(8,128)(2,1)}), bf16[16,1,136,128]{3,2,1,0:T(8,128)(2,1)S(1)}, u32[]{:S(2)}, u32[]{:S(2)}) async-start(bf16[16,1,136,128]{3,2,1,0:T(8,128)(2,1)} %bitcast.27), calls=%async_computation.6 | async-start | bytes 1114112 | tf_op jit(solution)/shard_map/all_to_all | solution.py:412
  214.2 18.6 %all-to-all-start.7 = ((bf16[32,8,384]{2,1,0:T(8,128)(2,1)}), bf16[32,8,384]{2,1,0:T(8,128)(2,1)S(1)}, u32[]{:S(2)}, u32[]{:S(2)}) async-start(bf16[32,8,384]{2,1,0:T(8,128)(2,1)} %bitcast.29), calls=%async_computation.7 | async-start | bytes 393216 | tf_op jit(solution)/shard_map/all_to_all | solution.py:412
